TPU v7x, 256 devices: a whole 4x4x8 slice. The times are simulated.
256 devices in a mesh: rep: 16 (over x, y_hi, core), hid: 16 (over y_lo, z).
Axes of the slice: x: 4, y: 4 (y_hi: 2, y_lo: 2; y = y_hi * 2 + y_lo), z: 8, core: 2. Of those that a mesh axis runs over, the one named last changes fastest.
Arguments:
- tokens: bfloat16 [2, 8192, 1152], P(None, ('rep', 'hid')), may hold values from -6 to 6
- targets: bfloat16 [2, 8192, 1152], P(None, ('rep', 'hid')), may hold values from -6 to 6
- w_gate: float32 [16, 6912, 1152], P('rep', 'hid'), may hold values from -6 to 6
- w_up: float32 [16, 6912, 1152], P('rep', 'hid'), may hold values from -6 to 6
- w_down: float32 [16, 6912, 1152], P('rep', 'hid'), may hold values from -6 to 6
Outputs:
- new_gate: float32 [16, 6912, 1152], P('rep', 'hid')
- new_up: float32 [16, 6912, 1152], P('rep', 'hid')
- new_down: float32 [16, 6912, 1152], P('rep', 'hid')
All inputs are finite; a program needn't handle non-finite values.
Results may differ from a plain program's by a relative error of at most 0.0086.
Values may be sent and summed in bfloat16 or wider, within the bound.
No kernel may reach another device: no remote copies, remote signals or barrier semaphores. Data moves between devices by JAX's collectives and lax.ppermute only.
A program may use at most 128 MiB of HBM per device.

v0:
```python
import jax
import jax.numpy as jnp
from jax import lax
from jax.sharding import PartitionSpec as P

D = 1152
FF = 6912
STEPS = 2
LEARNING_RATE = 0.5


def swapped(value, axis, distance):
    mask = 2**distance
    pairs = [(source, source ^ mask) for source in range(lax.axis_size(axis))]
    return lax.ppermute(value, axis, pairs)


def gelu_tanh(value):
    return jax.nn.gelu(value, approximate=True)


def contract_cols(left, right):
    return lax.dot_general(
        left, right, (((1,), (1,)), ((), ())), preferred_element_type=jnp.float32
    )


def contract_rows(left, right):
    return lax.dot_general(
        left, right, (((0,), (0,)), ((), ())), preferred_element_type=jnp.float32
    )


def local(tokens, targets, w_gate, w_up, w_down):
    scale_model = float(D) ** (-0.5)
    scale_hidden = float(FF) ** (-0.5)
    all_tokens, all_targets = (
        lax.all_gather(tokens, "hid", axis=1, tiled=True),
        lax.all_gather(targets, "hid", axis=1, tiled=True),
    )
    weights = (w_gate[0], w_up[0], w_down[0])
    for step_index in range(STEPS):
        token_batch = all_tokens[step_index]
        gate_half = weights[0].astype(jnp.bfloat16)
        up_half = weights[1].astype(jnp.bfloat16)
        down_half = weights[2].astype(jnp.bfloat16)
        gate_value = contract_cols(token_batch, gate_half) * scale_model
        up_value = contract_cols(token_batch, up_half) * scale_model
        activated, gelu_back = jax.vjp(gelu_tanh, gate_value)
        hidden = (activated * up_value).astype(jnp.bfloat16)
        partial_out = jnp.dot(hidden, down_half, preferred_element_type=jnp.float32) * scale_hidden
        output = lax.psum(partial_out, "hid")
        residual = (output - all_targets[step_index].astype(jnp.float32)).astype(jnp.bfloat16)
        grad_down = contract_rows(hidden, residual) * scale_hidden
        hidden_grad = contract_cols(residual, down_half) * scale_hidden
        gate_grad = gelu_back(hidden_grad * up_value)[0].astype(jnp.bfloat16)
        up_grad = (hidden_grad * activated).astype(jnp.bfloat16)
        grad_gate = contract_rows(gate_grad, token_batch) * scale_model
        grad_up = contract_rows(up_grad, token_batch) * scale_model
        gradients = (grad_gate, grad_up, grad_down)
        stepped = tuple(
            (weight - LEARNING_RATE * gradient for weight, gradient in zip(weights, gradients))
        )
        partner_new = swapped(stepped, "rep", step_index)
        weights = tuple(((mine + theirs) * 0.5 for mine, theirs in zip(stepped, partner_new)))
    return (weights[0][None], weights[1][None], weights[2][None])


def solution(mesh):
    placed = (
        P(None, ("rep", "hid"), None),
        P(None, ("rep", "hid"), None),
        P("rep", "hid", None),
        P("rep", "hid", None),
        P("rep", "hid", None),
    )
    return jax.shard_map(
        local,
        mesh=mesh,
        in_specs=placed,
        out_specs=(P("rep", "hid", None), P("rep", "hid", None), P("rep", "hid", None)),
        check_vma=False,
    )
```

profile of v0, /device:TPU:2, one launch (start us, length us, event | category | flops | bytes accessed | tf_op | source)
XLA Modules:
  0.0 596.4 jit_solution(7558475511796509803)
XLA Ops:
  7.2 0.7 all-gather.3.cloned.1.call-update
  7.9 0.0 all-gather.5.cloned.1.call-start
  7.9 0.7 all-gather.5.cloned.1.call-update
  8.6 0.0 all-reduce.3.cloned.1.call-start
  8.7 76.2 %all-gather.3.cloned.1.call-done = bf16[2,512,1152]{2,1,0:T(8,128)(2,1)} async-done(((bf16[2,32,1152]{2,1,0:T(8,128)(2,1)}), bf16[2,512,1152]{2,1,0:T(8,128)(2,1)}) %all-gather.3.cloned.1.call-update) | async-done | bytes 2359312 | tf_op jit(solution)/shard_map/all_gather | solution.py:38
  84.9 2.8 convolution_multiply_fusion.13
  87.7 3.5 multiply_convert_fusion.3
  91.2 0.8 copy-done.25
  92.0 2.3 convolution_multiply_fusion.1
  94.3 0.0 all-reduce.5.cloned.1.call-start
  94.4 61.8 %all-gather.5.cloned.1.call-done = bf16[2,512,1152]{2,1,0:T(8,128)(2,1)} async-done(((bf16[2,32,1152]{2,1,0:T(8,128)(2,1)}), bf16[2,512,1152]{2,1,0:T(8,128)(2,1)}) %all-gather.5.cloned.1.call-update) | async-done | bytes 2359312 | tf_op jit(solution)/shard_map/all_gather | solution.py:39
  156.2 143.4 %all-reduce.3.cloned.1.call-done = f32[512,1152]{1,0:T(8,128)} async-done(((f32[512,1152]{1,0:T(8,128)}), f32[512,1152]{1,0:T(8,128)}) %all-reduce.3.cloned.1.call-update) | async-done | bytes 2359312 | tf_op jit(solution)/shard_map/psum | solution.py:52
  299.6 3.5 convolution_multiply_fusion.11
  303.2 1.3 fusion.5
  304.5 0.1 collective-permute-start
  304.6 0.1 copy-done.4
  304.7 0.7 copy-done.8
  305.4 1.4 copy-done.9
  306.9 0.9 fusion.3
  307.8 0.1 collective-permute-start.2
  307.9 1.0 fusion.4
  308.8 0.6 collective-permute-start.1
  309.4 0.8 fusion.9
  310.2 0.5 copy-done.18
  310.8 1.1 collective-permute-done.2
  311.9 0.3 fusion.30
  312.2 1.1 copy-done.16
  313.2 1.5 collective-permute-done.1
  314.7 1.9 multiply_convert_fusion.1
  316.6 0.8 copy-done.20
  317.4 2.3 convolution_multiply_fusion
  319.7 140.9 %all-reduce.5.cloned.1.call-done = f32[512,1152]{1,0:T(8,128)} async-done(((f32[512,1152]{1,0:T(8,128)}), f32[512,1152]{1,0:T(8,128)}) %all-reduce.5.cloned.1.call-update) | async-done | bytes 2359312 | tf_op jit(solution)/shard_map/psum | solution.py:52
  460.6 3.2 convolution_multiply_fusion.8
  463.8 0.3 copy-done.13
  464.2 1.0 fusion.1
  465.2 3.5 collective-permute-start.4
  468.7 1.4 fusion.2
  470.1 1.1 collective-permute-start.3
  471.2 0.4 copy-done.10
  471.6 0.6 copy-done.17
  472.2 0.9 fusion
  473.1 1.6 collective-permute-start.5
  474.7 38.5 %collective-permute-done.4 = f32[432,1152]{1,0:T(8,128)S(1)} collective-permute-done((f32[432,1152]{1,0:T(8,128)S(1)}, f32[432,1152]{1,0:T(8,128)S(1)}, u32[]{:S(2)}, u32[]{:S(2)}) %collective-permute-start.4) | collective-permute-done | bytes 1990688 | tf_op jit(solution)/shard_map/ppermute | solution.py:15
  513.2 1.6 multiply_bitcast_fusion.1
  514.7 41.1 %collective-permute-done.3 = f32[432,1152]{1,0:T(8,128)S(1)} collective-permute-done((f32[432,1152]{1,0:T(8,128)S(1)}, f32[432,1152]{1,0:T(8,128)S(1)}, u32[]{:S(2)}, u32[]{:S(2)}) %collective-permute-start.3) | collective-permute-done | bytes 1990688 | tf_op jit(solution)/shard_map/ppermute | solution.py:15
  555.8 1.6 multiply_bitcast_fusion.2
  557.4 31.0 %collective-permute-done.5 = f32[432,1152]{1,0:T(8,128)S(1)} collective-permute-done((f32[432,1152]{1,0:T(8,128)S(1)}, f32[432,1152]{1,0:T(8,128)S(1)}, u32[]{:S(2)}, u32[]{:S(2)}) %collective-permute-start.5) | collective-permute-done | bytes 1990688 | tf_op jit(solution)/shard_map/ppermute | solution.py:15
  588.4 1.6 multiply_bitcast_fusion
  (50 shorter events, 0.2 us)
Async XLA Ops:
  7.2 77.7 %all-gather.3.cloned.1.call-start = ((), (), s32[]{:S(2)}) async-start(), calls=%async_computation | async-start | bytes 2506752 | tf_op jit(solution)/shard_map/all_gather | solution.py:38
  7.9 148.3 %all-gather.5.cloned.1.call-start = ((), (), s32[]{:S(2)}) async-start(), calls=%async_computation.2 | async-start | bytes 2506752 | tf_op jit(solution)/shard_map/all_gather | solution.py:39
  8.6 290.9 %all-reduce.3.cloned.1.call-start = ((), (), s32[]{:S(2)}) async-start(), calls=%async_computation.1 | async-start | bytes 4718592 | tf_op jit(solution)/shard_map/psum | solution.py:52
  84.9 2.8 copy-start
  87.7 4.3 copy-start.3
  91.2 0.8 copy-start.25
  94.3 366.3 %all-reduce.5.cloned.1.call-start = ((), (), s32[]{:S(2)}) async-start(), calls=%async_computation.3 | async-start | bytes 4718592 | tf_op jit(solution)/shard_map/psum | solution.py:52
  299.6 3.6 copy-start.23
  299.6 3.6 copy-start.27
  303.2 1.6 copy-start.4
  303.2 2.3 copy-start.8
  303.2 3.7 copy-start.9
  303.2 3.7 copy-start.26
  304.5 4.9 copy-start.14
  304.5 3.3 copy-start.24
  304.5 4.9 collective-permute-start
  307.7 4.1 copy-start.5
  307.8 4.1 collective-permute-start.2
  308.8 5.9 copy-start.1
  308.8 5.9 collective-permute-start.1
  309.4 1.3 copy-start.18
  311.9 1.4 copy-start.16
  313.2 3.4 copy-start.11
  314.7 1.9 copy-start.12
  316.6 0.8 copy-start.20
  460.6 3.2 copy-start.2
  460.6 3.5 copy-start.13
  464.1 4.5 copy-start.15
  464.1 4.5 copy-start.19
  464.1 4.5 copy-start.22
  465.2 48.0 %collective-permute-start.4 = (f32[432,1152]{1,0:T(8,128)S(1)}, f32[432,1152]{1,0:T(8,128)S(1)}, u32[]{:S(2)}, u32[]{:S(2)}) collective-permute-start(f32[432,1152]{1,0:T(8,128)S(1)} %fusion.1), channel_id=1, source_target_pairs={{0,32},{16,48},{32,0},{48,16},{64,96},{80,112},{96,64},{112,80},{1... | collective-permute-start | bytes 5971976 | tf_op jit(solution)/shard_map/ppermute | solution.py:15
  468.6 2.5 copy-start.6
  468.7 2.5 copy-start.7
  468.7 3.0 copy-start.10
  468.7 3.5 copy-start.17
  468.7 3.5 copy-start.21
  470.1 85.8 %collective-permute-start.3 = (f32[432,1152]{1,0:T(8,128)S(1)}, f32[432,1152]{1,0:T(8,128)S(1)}, u32[]{:S(2)}, u32[]{:S(2)}) collective-permute-start(f32[432,1152]{1,0:T(8,128)S(1)} %fusion.2), channel_id=1, source_target_pairs={{0,32},{16,48},{32,0},{48,16},{64,96},{80,112},{96,64},{112,80},{1... | collective-permute-start | bytes 5971976 | tf_op jit(solution)/shard_map/ppermute | solution.py:15
  473.1 115.2 %collective-permute-start.5 = (f32[432,1152]{1,0:T(8,128)S(1)}, f32[432,1152]{1,0:T(8,128)S(1)}, u32[]{:S(2)}, u32[]{:S(2)}) collective-permute-start(f32[432,1152]{1,0:T(8,128)S(1)} %fusion), channel_id=1, source_target_pairs={{0,32},{16,48},{32,0},{48,16},{64,96},{80,112},{96,64},{112,80},{1... | collective-permute-start | bytes 5971976 | tf_op jit(solution)/shard_map/ppermute | solution.py:15
Sparse Core Ops, SparseCore 0:
  9.8 75.0 all-gather.2
  86.7 69.5 all-gather.4
  158.9 140.6 all-reduce.2
  319.8 140.7 all-reduce.4
where the time goes:
time: 597 us; the launch traced here: 596 us
  waiting for transfers between devices  537 us (90%)
  matrix products  26.8 us (4%)
  between operations  14 us (2%)
  starting transfers between devices  7.08 us (1%)
  local copies, waits for them, and re-layouts  6.79 us (1%)
    psum x2, waiting for transfers between devices, local(): output = lax.psum(partial_out, 'hid')  284 us
    ppermute x6, waiting for transfers between devices, swapped(): return lax.ppermute(value, axis, pairs)  113 us
    all_gather x1, waiting for transfers between devices, local(): lax.all_gather(tokens, 'hid', axis=1, tiled=True)  76.2 us
    all_gather x1, waiting for transfers between devices, local(): lax.all_gather(targets, 'hid', axis=1, tiled=True)  61.8 us
    dot_general x6, matrix products, contract_cols(): lax.dot_general(left, right, (((1,), (1,)), ((), ())), preferred_element_...  15.8 us
  transfers between devices with their start and end apart: 10, of which 9 were waited for; matrix products, arithmetic and copies ran while one was open for 3% of the time, Pallas kernels for 0%

commit v1 on v0

--- a/solution.py
+++ b/solution.py
@@ -49,7 +49,7 @@
         activated, gelu_back = jax.vjp(gelu_tanh, gate_value)
         hidden = (activated * up_value).astype(jnp.bfloat16)
         partial_out = jnp.dot(hidden, down_half, preferred_element_type=jnp.float32) * scale_hidden
-        output = lax.psum(partial_out, "hid")
+        output = jnp.sum(lax.all_gather(partial_out, "hid"), axis=0)
         residual = (output - all_targets[step_index].astype(jnp.float32)).astype(jnp.bfloat16)
         grad_down = contract_rows(hidden, residual) * scale_hidden
         hidden_grad = contract_cols(residual, down_half) * scale_hidden

time: 597 us -> 1130 us (1.89)
  waiting for transfers between devices: 537 us -> 1040 us
  other arithmetic: 4.99 us -> 34.2 us
    all_gather x0 -> x2, waiting for transfers between devices: none -> 786 us  [local(): output = jnp.sum(lax.all_gather(partial_out, 'hid'), axis=0)]
    psum x2 -> x0, waiting for transfers between devices: 284 us -> none  [local(): output = lax.psum(partial_out, 'hid')]
    reduce_sum x0 -> x2, other arithmetic: none -> 29.2 us  [local(): output = jnp.sum(lax.all_gather(partial_out, 'hid'), axis=0)]
  transfers between devices with their start and end apart: 10 -> 10, of which waited for: 9 -> 9; matrix products, arithmetic and copies ran while one was open for 3% -> 2% of each run, Pallas kernels for 0% -> 0%
where the time goes in v1:
time: 1130 us
  waiting for transfers between devices  1040 us (92%)
  other arithmetic  34.2 us (3%)
  matrix products  26.8 us (2%)
  between operations  14 us (1%)
    all_gather x2, waiting for transfers between devices, local(): output = jnp.sum(lax.all_gather(partial_out, 'hid'), axis=0)  786 us
    ppermute x6, waiting for transfers between devices, swapped(): return lax.ppermute(value, axis, pairs)  122 us
    all_gather x1, waiting for transfers between devices, local(): lax.all_gather(tokens, 'hid', axis=1, tiled=True)  76.9 us
    all_gather x1, waiting for transfers between devices, local(): lax.all_gather(targets, 'hid', axis=1, tiled=True)  57 us
    reduce_sum x2, other arithmetic, local(): output = jnp.sum(lax.all_gather(partial_out, 'hid'), axis=0)  29.2 us
  transfers between devices with their start and end apart: 10, of which 9 were waited for; matrix products, arithmetic and copies ran while one was open for 2% of the time, Pallas kernels for 0%

profile of v1, /device:TPU:2, one launch (start us, length us, event | category | flops | bytes accessed | tf_op | source)
XLA Modules:
  0.0 1132.0 jit_solution(12868495556848640955)
XLA Ops:
  7.2 0.7 all-gather.7.cloned.1.call-update
  7.9 76.9 %all-gather.7.cloned.1.call-done = bf16[2,512,1152]{2,1,0:T(8,128)(2,1)} async-done(((bf16[2,32,1152]{2,1,0:T(8,128)(2,1)}), bf16[2,512,1152]{2,1,0:T(8,128)(2,1)}) %all-gather.7.cloned.1.call-update) | async-done | bytes 2359312 | tf_op jit(solution)/shard_map/all_gather | solution.py:38
  84.9 2.8 convolution_multiply_fusion.13
  87.7 3.5 multiply_convert_fusion.3
  91.2 0.8 copy-done.25
  92.0 2.3 convolution_multiply_fusion.1
  94.3 0.0 all-gather.9.cloned.1.call-start
  94.4 0.7 all-gather.9.cloned.1.call-update
  95.1 392.7 %all-gather.11.cloned.1.call-done = f32[8192,1152]{1,0:T(8,128)} async-done(((f32[512,1152]{1,0:T(8,128)}), f32[8192,1152]{1,0:T(8,128)}) %all-gather.11.cloned.1.call-update) | async-done | bytes 37748752 | tf_op jit(solution)/shard_map/all_gather | solution.py:52
  487.8 14.6 %reduce_sum.20 = f32[512,1152]{1,0:T(8,128)} reduce(f32[16,512,1152]{2,1,0:T(8,128)} %bitcast.84, f32[]{:T(128)} %constant.26.clone.1), dimensions={0}, to_apply=%region_0.0 | reduce | flops 8847360 | bytes 40108036 | tf_op jit(solution)/shard_map/reduce_sum | solution.py:52
  502.4 57.0 %all-gather.9.cloned.1.call-done = bf16[2,512,1152]{2,1,0:T(8,128)(2,1)} async-done(((bf16[2,32,1152]{2,1,0:T(8,128)(2,1)}), bf16[2,512,1152]{2,1,0:T(8,128)(2,1)}) %all-gather.9.cloned.1.call-update) | async-done | bytes 2359312 | tf_op jit(solution)/shard_map/all_gather | solution.py:39
  559.4 3.5 convolution_multiply_fusion.11
  563.0 1.3 fusion.5
  564.3 0.1 collective-permute-start
  564.4 0.2 copy-done.2
  564.6 0.6 copy-done.6
  565.2 1.4 copy-done.9
  566.7 0.9 fusion.3
  567.6 0.1 collective-permute-start.2
  567.7 1.0 fusion.4
  568.6 0.8 collective-permute-start.1
  569.4 0.8 fusion.11
  570.2 0.5 copy-done.18
  570.7 1.0 collective-permute-done.2
  571.7 0.3 fusion.39
  572.0 1.0 copy-done.16
  573.0 1.5 collective-permute-done.1
  574.5 1.9 multiply_convert_fusion.1
  576.4 0.8 copy-done.20
  577.2 2.3 convolution_multiply_fusion
  579.5 393.4 %all-gather.13.cloned.1.call-done = f32[8192,1152]{1,0:T(8,128)} async-done(((f32[512,1152]{1,0:T(8,128)}), f32[8192,1152]{1,0:T(8,128)}) %all-gather.13.cloned.1.call-update) | async-done | bytes 37748752 | tf_op jit(solution)/shard_map/all_gather | solution.py:52
  973.0 14.6 %reduce_sum.22 = f32[512,1152]{1,0:T(8,128)} reduce(f32[16,512,1152]{2,1,0:T(8,128)} %bitcast.85, f32[]{:T(128)} %constant.26.clone.1), dimensions={0}, to_apply=%region_1.0 | reduce | flops 8847360 | bytes 40108036 | tf_op jit(solution)/shard_map/reduce_sum | solution.py:52
  987.6 3.2 convolution_multiply_fusion.8
  990.8 0.3 copy-done.13
  991.1 1.0 fusion.1
  992.1 2.8 collective-permute-start.4
  995.0 1.4 fusion.2
  996.3 1.3 collective-permute-start.3
  997.7 0.3 copy-done.10
  997.9 0.6 copy-done.17
  998.5 0.9 fusion
  999.4 1.6 collective-permute-start.5
  1001.0 38.9 %collective-permute-done.4 = f32[432,1152]{1,0:T(8,128)S(1)} collective-permute-done((f32[432,1152]{1,0:T(8,128)S(1)}, f32[432,1152]{1,0:T(8,128)S(1)}, u32[]{:S(2)}, u32[]{:S(2)}) %collective-permute-start.4) | collective-permute-done | bytes 1990688 | tf_op jit(solution)/shard_map/ppermute | solution.py:15
  1039.9 1.6 multiply_bitcast_fusion.1
  1041.5 41.1 %collective-permute-done.3 = f32[432,1152]{1,0:T(8,128)S(1)} collective-permute-done((f32[432,1152]{1,0:T(8,128)S(1)}, f32[432,1152]{1,0:T(8,128)S(1)}, u32[]{:S(2)}, u32[]{:S(2)}) %collective-permute-start.3) | collective-permute-done | bytes 1990688 | tf_op jit(solution)/shard_map/ppermute | solution.py:15
  1082.6 1.6 multiply_bitcast_fusion.2
  1084.2 39.8 %collective-permute-done.5 = f32[432,1152]{1,0:T(8,128)S(1)} collective-permute-done((f32[432,1152]{1,0:T(8,128)S(1)}, f32[432,1152]{1,0:T(8,128)S(1)}, u32[]{:S(2)}, u32[]{:S(2)}) %collective-permute-start.5) | collective-permute-done | bytes 1990688 | tf_op jit(solution)/shard_map/ppermute | solution.py:15
  1124.0 1.6 multiply_bitcast_fusion
  (52 shorter events, 0.3 us)
Async XLA Ops:
  7.2 77.7 %all-gather.7.cloned.1.call-start = ((), (), s32[]{:S(2)}) async-start(), calls=%async_computation | async-start | bytes 2506752 | tf_op jit(solution)/shard_map/all_gather | solution.py:38
  7.9 479.9 %all-gather.11.cloned.1.call-start = ((), (), s32[]{:S(2)}) async-start(), calls=%async_computation.2 | async-start | bytes 40108032 | tf_op jit(solution)/shard_map/all_gather | solution.py:52
  84.9 2.8 copy-start
  87.7 4.3 copy-start.5
  91.2 0.8 copy-start.25
  94.3 465.1 %all-gather.9.cloned.1.call-start = ((), (), s32[]{:S(2)}) async-start(), calls=%async_computation.1 | async-start | bytes 2506752 | tf_op jit(solution)/shard_map/all_gather | solution.py:39
  95.1 877.9 %all-gather.13.cloned.1.call-start = ((), (), s32[]{:S(2)}) async-start(), calls=%async_computation.3 | async-start | bytes 40108032 | tf_op jit(solution)/shard_map/all_gather | solution.py:52
  559.4 3.6 copy-start.23
  559.4 3.6 copy-start.27
  563.0 1.7 copy-start.2
  563.0 2.3 copy-start.6
  563.0 3.7 copy-start.9
  563.0 3.7 copy-start.26
  564.3 5.1 copy-start.14
  564.3 3.3 copy-start.24
  564.3 5.1 collective-permute-start
  567.5 4.1 copy-start.7
  567.6 4.1 collective-permute-start.2
  568.6 5.9 copy-start.3
  568.6 5.9 collective-permute-start.1
  569.4 1.3 copy-start.18
  571.7 1.3 copy-start.16
  573.0 3.5 copy-start.11
  574.5 1.9 copy-start.12
  576.4 0.8 copy-start.20
  987.6 3.2 copy-start.4
  987.6 3.5 copy-start.13
  991.1 3.8 copy-start.15
  991.1 3.8 copy-start.19
  991.1 3.8 copy-start.22
  992.1 47.8 %collective-permute-start.4 = (f32[432,1152]{1,0:T(8,128)S(1)}, f32[432,1152]{1,0:T(8,128)S(1)}, u32[]{:S(2)}, u32[]{:S(2)}) collective-permute-start(f32[432,1152]{1,0:T(8,128)S(1)} %fusion.1), channel_id=1, source_target_pairs={{0,32},{16,48},{32,0},{48,16},{64,96},{80,112},{96,64},{112,80},{1... | collective-permute-start | bytes 5971976 | tf_op jit(solution)/shard_map/ppermute | solution.py:15
  994.9 2.7 copy-start.1
  994.9 2.7 copy-start.8
  995.0 3.0 copy-start.10
  995.0 3.5 copy-start.17
  995.0 3.5 copy-start.21
  996.3 86.2 %collective-permute-start.3 = (f32[432,1152]{1,0:T(8,128)S(1)}, f32[432,1152]{1,0:T(8,128)S(1)}, u32[]{:S(2)}, u32[]{:S(2)}) collective-permute-start(f32[432,1152]{1,0:T(8,128)S(1)} %fusion.2), channel_id=1, source_target_pairs={{0,32},{16,48},{32,0},{48,16},{64,96},{80,112},{96,64},{112,80},{1... | collective-permute-start | bytes 5971976 | tf_op jit(solution)/shard_map/ppermute | solution.py:15
  999.4 124.5 %collective-permute-start.5 = (f32[432,1152]{1,0:T(8,128)S(1)}, f32[432,1152]{1,0:T(8,128)S(1)}, u32[]{:S(2)}, u32[]{:S(2)}) collective-permute-start(f32[432,1152]{1,0:T(8,128)S(1)} %fusion), channel_id=1, source_target_pairs={{0,32},{16,48},{32,0},{48,16},{64,96},{80,112},{96,64},{112,80},{1... | collective-permute-start | bytes 5971976 | tf_op jit(solution)/shard_map/ppermute | solution.py:15
Sparse Core Ops, SparseCore 0:
  9.8 75.0 all-gather.6
  94.5 393.2 all-gather.10
  489.6 69.7 all-gather.8
  579.6 393.2 all-gather.12
